TPU v7x, 1024 devices: a whole 8x8x8 slice. The times are simulated.
1024 devices in a mesh: dp: 128 (over x, z_hi, y), fsdp: 8 (over z_lo, core).
Axes of the slice: x: 8, y: 8, z: 8 (z_hi: 2, z_lo: 4; z = z_hi * 4 + z_lo), core: 2. Of those that a mesh axis runs over, the one named last changes fastest.
Arguments:
- features: bfloat16 [2048, 14, 14, 1, 512], P(('dp', 'fsdp')), may hold values from -17 to 17
- conv_weight: bfloat16 [1, 4608, 512], P(None, None, 'fsdp'), may hold values from -0.09375 to 0.09375
- proj_weight: bfloat16 [512, 256], replicated, may hold values from -0.5745243 to 0.5745243
- prototypes: bfloat16 [256, 3072], P(None, 'fsdp'), may hold values from -72 to 72
Outputs:
- codes: float32 [2048, 3072], P(('dp', 'fsdp'))
All inputs are finite; a program needn't handle non-finite values.
Results may differ from a plain program's by a relative error of at most 0.008.
Values may be sent and summed in bfloat16 or wider, within the bound.
A program may use at most 32 MiB of HBM per device.

v0:
```python
import jax
import jax.numpy as jnp
from jax import lax
from jax.sharding import PartitionSpec as P

SINK = 3


logit_sharpening_divisor = 0.05
epsilon_norm = 1e-06


def conv_pool(images, kernel, residual):
    img_count, side_len, _, group_count, group_width = images.shape
    padded = jnp.pad(images, ((0, 0), (1, 1), (1, 1), (0, 0), (0, 0)))
    running = jnp.zeros(images.shape[:4] + (kernel.shape[2],), jnp.float32)
    for tap_index in range(9):
        row_offset, col_shift = divmod(tap_index, 3)
        window = padded[:, row_offset : row_offset + side_len, col_shift : col_shift + side_len]
        tap_weights = kernel[:, tap_index * group_width : (tap_index + 1) * group_width, :]
        running = running + jnp.einsum(
            "bhwgi,gio->bhwgo", window, tap_weights, preferred_element_type=jnp.float32
        )
    rectified_output = jax.nn.relu(running + residual.astype(jnp.float32))
    return jnp.mean(rectified_output, axis=(1, 2))


def unit_columns(protos_half):
    protos_wide = protos_half.astype(jnp.float32)
    return (
        protos_wide
        / jnp.sqrt(jnp.sum(protos_wide * protos_wide, axis=0, keepdims=True) + epsilon_norm)
    ).astype(jnp.bfloat16)


def shards(features, conv_weight, proj_weight, prototypes):
    img_count = features.shape[0]
    pooled = conv_pool(features, lax.all_gather(conv_weight, "fsdp", axis=2, tiled=True), features)
    pooled = pooled.reshape(img_count, -1)
    projected = jnp.dot(
        pooled.astype(jnp.bfloat16), proj_weight, preferred_element_type=jnp.float32
    )
    image_embedding = (
        projected / jnp.sqrt(jnp.sum(projected * projected, axis=1, keepdims=True) + epsilon_norm)
    ).astype(jnp.bfloat16)
    every_proto = lax.all_gather(prototypes, "fsdp", axis=1, tiled=True)
    normalized_prototypes = unit_columns(every_proto)
    cluster_center_count = normalized_prototypes.shape[1]
    probabilistic_cluster_share = jnp.exp(
        jnp.dot(image_embedding, normalized_prototypes, preferred_element_type=jnp.float32)
        / logit_sharpening_divisor
    )
    for sweep in range(SINK):
        prototype_sums = lax.psum(jnp.sum(probabilistic_cluster_share, axis=0), ("dp", "fsdp"))
        probabilistic_cluster_share = probabilistic_cluster_share / prototype_sums[None, :]
        probabilistic_cluster_share = probabilistic_cluster_share / jnp.sum(
            probabilistic_cluster_share, axis=1, keepdims=True
        )
    return cluster_center_count * probabilistic_cluster_share


def solution(mesh):
    return jax.shard_map(
        shards,
        mesh=mesh,
        in_specs=(
            P(("dp", "fsdp"), None, None, None, None),
            P(None, None, "fsdp"),
            P(),
            P(None, "fsdp"),
        ),
        out_specs=P(("dp", "fsdp"), None),
        check_vma=False,
    )
```

profile of v0, /device:TPU:1, one launch (start us, length us, event | category | flops | bytes accessed | tf_op | source)
XLA Modules:
  0.0 486.6 jit_solution(6685648245680383007)
XLA Ops:
  6.5 0.7 all-gather.5.cloned.1.call-update
  7.3 0.7 all-gather.3.cloned.1.call-update
  8.0 1.1 copy.9
  9.1 55.8 %all-gather.5.cloned.1.call-done = bf16[256,3072]{1,0:T(8,128)(2,1)} async-done(((bf16[256,384]{1,0:T(8,128)(2,1)}), bf16[256,3072]{1,0:T(8,128)(2,1)}) %all-gather.5.cloned.1.call-update) | async-done | bytes 1572880 | tf_op jit(solution)/shard_map/all_gather | solution.py:46
  64.9 1.7 fusion.1
  66.6 64.7 %all-gather.3.cloned.1.call-done = bf16[1,4608,512]{1,2,0:T(8,128)(2,1)} async-done(((bf16[1,4608,64]{1,2,0:T(8,128)(2,1)}), bf16[1,4608,512]{1,2,0:T(8,128)(2,1)}) %all-gather.3.cloned.1.call-update) | async-done | bytes 4718608 | tf_op jit(solution)/shard_map/all_gather | solution.py:38
  131.3 1.6 fusion.13
  133.0 1.5 convolution_add_fusion.3
  134.4 1.5 convolution_add_fusion.2
  136.0 0.4 fusion.9
  136.4 0.4 convolution_add_fusion
  136.8 0.4 fusion.8
  137.3 0.4 fusion.7
  137.8 0.4 fusion.6
  138.2 0.5 fusion.12
  138.7 0.3 multiply_reduce_fusion
  139.0 0.4 fusion.57
  139.4 117.8 %psum.21 = f32[3072]{0:T(1024)S(1)} all-reduce(f32[3072]{0:T(1024)S(1)} %get-tuple-element.7), channel_id=1, replica_groups=mesh['dp'=128,'fsdp'=8] {'dp','fsdp'}, use_global_device_ids=true, to_apply=%region_4.5 | all-reduce | flops 3072 | bytes 24576 | tf_op jit(solution)/shard_map/psum | solution.py:54
  257.2 0.1 divide_reduce_fusion
  257.5 110.3 %psum.22 = f32[3072]{0:T(1024)S(1)} all-reduce(f32[3072]{0:T(1024)S(1)} %fusion.41), channel_id=1, replica_groups=mesh['dp'=128,'fsdp'=8] {'dp','fsdp'}, use_global_device_ids=true, to_apply=%region_7.8 | all-reduce | flops 3072 | bytes 24576 | tf_op jit(solution)/shard_map/psum | solution.py:54
  367.8 0.2 fusion.42
  368.1 110.7 %psum.23 = f32[3072]{0:T(1024)S(1)} all-reduce(f32[3072]{0:T(1024)S(1)} %divide_reduce_fusion.1), channel_id=1, replica_groups=mesh['dp'=128,'fsdp'=8] {'dp','fsdp'}, use_global_device_ids=true, to_apply=%region_10.11 | all-reduce | flops 3072 | bytes 24576 | tf_op jit(solution)/shard_map/psum | solution.py:54
  478.8 0.2 divide_reduce_fusion.2
  479.0 0.7 fusion.43
  (14 shorter events, 0.3 us)
Async XLA Ops:
  6.5 132.2 %copy-start = (bf16[512,256]{1,0:T(8,128)(2,1)S(1)}, bf16[512,256]{1,0:T(8,128)(2,1)}, u32[]{:S(2)}) copy-start(bf16[512,256]{1,0:T(8,128)(2,1)} %param.6) | copy-start | bytes 786436
  6.5 58.3 %all-gather.5.cloned.1.call-start = ((), (), s32[]{:S(2)}) async-start(), calls=%async_computation.1 | async-start | bytes 1769472 | tf_op jit(solution)/shard_map/all_gather | solution.py:46
  7.3 124.1 %all-gather.3.cloned.1.call-start = ((), (), s32[]{:S(2)}) async-start(), calls=%async_computation | async-start | bytes 5308416 | tf_op jit(solution)/shard_map/all_gather | solution.py:38
  66.6 69.8 %copy-start.2 = (bf16[2,14,14,1,512]{4,0,3,2,1:T(2,128)(2,1)S(1)}, bf16[2,14,14,1,512]{4,0,3,2,1:T(2,128)(2,1)}, u32[]{:S(2)}) copy-start(bf16[2,14,14,1,512]{4,0,3,2,1:T(2,128)(2,1)} %param.4) | copy-start | bytes 1204228
  131.3 4.6 copy-start.1
  137.3 1.7 copy-start.3
Sparse Core Ops, SparseCore 0:
  10.0 54.7 all-gather.4
  67.5 63.7 all-gather.2
where the time goes:
time: 487 us
  blocking collectives  339 us (70%)
  waiting for transfers between devices  122 us (25%)
  between operations  13.5 us (3%)
  matrix products  7.98 us (2%)
    psum x3, blocking collectives, shards(): lax.psum(jnp.sum(probabilistic_cluster_share, axis=0), ('dp', 'fsdp'))  339 us
    all_gather x1, waiting for transfers between devices, shards(): lax.all_gather(conv_weight, 'fsdp', axis=2, tiled=True)  64.7 us
    all_gather x1, waiting for transfers between devices, shards(): every_proto = lax.all_gather(prototypes, 'fsdp', axis=1, tiled=True)  55.8 us
  transfers between devices with their start and end apart: 2, of which 2 were waited for; matrix products, arithmetic and copies ran while one was open for 1% of the time, Pallas kernels for 0%

commit v1 on v0

v1 whole, which is shorter than its diff:
```python
import jax
import jax.numpy as jnp
from jax import lax
from jax.experimental import pallas as pl
from jax.experimental.pallas import tpu as pltpu
from jax.sharding import PartitionSpec as P

MESH = pl.DeviceIdType.MESH
F32 = jnp.float32
BF16 = jnp.bfloat16

SINK = 3
PROTOS = 3072
EPS = 1e-06
TEMP = 0.05

N = 8
ROWS = 32
MAP = 14 * ROWS
KQ = 1152
HALF = PROTOS // 2
SLICE = 384


def device(x, y, z, c):
    dp = lax.rem(x, N) * 16 + (lax.rem(z, N) // 4) * 8 + lax.rem(y, N)
    return dp, lax.rem(z, 4) * 2 + lax.rem(c, 2)


def nt(a, b):
    return lax.dot_general(a, b, (((1,), (1,)), ((), ())), preferred_element_type=F32)


def split_rows(v):
    hi = v.astype(BF16).astype(F32)
    row = lax.broadcasted_iota(jnp.int32, (16, v.shape[1]), 0)
    return jnp.where(row == 0, hi, jnp.where(row == 1, v - hi, 0.0)).astype(BF16)


def kernel(
    x_hbm, w_hbm, proj_hbm, proto_hbm, out_ref,
    wide, sib, xf, xs, acc, gath, proj, proto, prs, part, zb, yb, ef, ehi, elo, cb, rb, fin,
    loc, sib_s, sib_r, p1_s, p1_r, p2_s, p2_r, pr_s, pr_r, pt_s, pt_r,
    d1_s, d1_r, d2_s, d2_r, c_s, c_r, r_s, r_r, f_s, f_r,
):
    dp, fs = lax.axis_index("dp"), lax.axis_index("fsdp")
    x, y, zh = dp // 16, lax.rem(dp, 8), lax.rem(dp // 8, 2)
    zl, c = fs // 2, lax.rem(fs, 2)
    z = zh * 4 + zl
    sibling = device(x, y, z, c + 1)
    zpeer = [None] + [device(x, y, z + k, c) for k in range(1, N)]
    ypeer = [None] + [device(x, y + k, z, c) for k in range(1, N)]
    xpeer = [None] + [device(x + k, y, z, c) for k in range(1, N)]

    def send(src, dst, s, r, to):
        pltpu.make_async_remote_copy(
            src_ref=src, dst_ref=dst, send_sem=s, recv_sem=r, device_id=to, device_id_type=MESH
        ).start()

    def wait(ref, sem):
        pltpu.make_async_copy(ref, ref, sem).wait()

    own = pl.ds(pl.multiple_of(zl * 64, 64), 64)
    for q in range(4):
        pltpu.make_async_copy(
            w_hbm.at[:, pl.ds(q * KQ, KQ)], gath.at[own, pl.ds(q * KQ, KQ)], loc.at[0]
        ).start()
    pltpu.make_async_copy(proto_hbm, proto, loc.at[1]).start()
    pltpu.make_async_copy(x_hbm, wide, loc.at[2]).start()
    pltpu.make_async_copy(proj_hbm, proj, loc.at[3]).start()

    barrier = pltpu.get_barrier_semaphore()
    for to in [sibling] + zpeer[1:] + ypeer[1:] + xpeer[1:]:
        pl.semaphore_signal(barrier, inc=1, device_id=to, device_id_type=MESH)

    pltpu.make_async_copy(proto_hbm, proto, loc.at[1]).wait()
    pw = proto[...].astype(F32)
    norm = jnp.sqrt(jnp.sum(pw * pw, axis=0, keepdims=True) + EPS)
    prs[zl] = (pw / norm).astype(BF16)
    pltpu.make_async_copy(x_hbm, wide, loc.at[2]).wait()
    wait(gath.at[pl.ds(0, 64), :], loc.at[0])

    pl.semaphore_wait(barrier, 1 + 3 * (N - 1))

    color = [lax.rem(x + 2 * y, 4), lax.rem(2 * x + y, 4)]

    def piece(s, h, g=None):
        row = s * 64 + h * 32
        rows = pl.ds(pl.multiple_of(row, 32), 32)
        if g is not None:
            rows = pl.ds(pl.multiple_of(row + 16 * g, 16), 16)
        return gath.at[rows, pl.ds(pl.multiple_of(color[h] * KQ, 128), KQ)]

    for h in range(2):
        mine = piece(zl, h)
        send(mine, mine, p1_s, p1_r.at[0, h], zpeer[7])
        send(mine, mine, p1_s, p1_r.at[2, h], zpeer[1])
    for h in range(2):
        for g, k in ((0, 2), (1, 6)):
            mine = piece(zl, h, g)
            send(mine, mine, p1_s, p1_r.at[1, h], zpeer[k])
    send(wide, sib, sib_s, sib_r, sibling)

    def spread(src, slot):
        xf[pl.ds(0, 48), :] = jnp.zeros((48, 512), F32)
        xf[pl.ds(48, MAP), :] = src[...].astype(F32)
        xf[pl.ds(48 + MAP, 48), :] = jnp.zeros((48, 512), F32)
        for j in range(3):
            xs[slot, j] = xf[pl.ds(14 + 2 * j, 512), :].astype(BF16)

    spread(wide, c)

    def forward(k, h):
        s = lax.rem(zl + k, 4)
        full, part_ = (xpeer, ypeer) if h == 0 else (ypeer, xpeer)
        wait(piece(s, h), p1_r.at[k - 1, h])
        for to in (full[1], full[7]):
            send(piece(s, h), piece(s, h), p2_s, p2_r, to)
        for g, to in ((0, part_[1]), (1, part_[7])):
            send(piece(s, h, g), piece(s, h, g), p2_s, p2_r, to)

    for k in (1, 3, 2):
        for h in range(2):
            forward(k, h)

    for to in (zpeer[1], zpeer[7]):
        send(prs.at[zl], prs.at[zl], pr_s, pr_r, to)
    for g, to in ((0, zpeer[2]), (1, zpeer[6])):
        rows = pl.ds(128 * g, 128)
        send(prs.at[zl, rows], prs.at[zl, rows], pr_s, pr_r, to)

    wait(sib, sib_r)
    spread(sib, 1 - c)

    o = lax.broadcasted_iota(jnp.int32, (256, 512), 0)
    i = lax.broadcasted_iota(jnp.int32, (256, 512), 1)
    pick = jnp.where(i == (o // 64) * 128 + 64 * c + lax.rem(o, 64), 1.0, 0.0).astype(BF16)
    for slot in range(2):
        acc[slot] = nt(xs[slot, 1, pl.ds(32, MAP), :], pick)

    wait(gath.at[pl.ds(0, 144), :], p2_r)

    def conv(slot, carry):
        for t in range(9):
            r, j = divmod(t, 3)
            acc[slot] += nt(xs[slot, j, pl.ds(32 * r, MAP), :], gath[:, pl.ds(512 * t, 512)])
        return carry

    lax.fori_loop(0, 2, conv, 0)

    row32 = lax.broadcasted_iota(jnp.int32, (ROWS, 256), 0)
    row16 = lax.broadcasted_iota(jnp.int32, (16, 256), 0)
    pooled = jnp.zeros((16, 256), F32)
    for slot in range(2):
        line = jnp.sum(jnp.maximum(acc[slot].reshape(14, ROWS, 256), 0.0), axis=0)
        for b in range(2):
            keep = (lax.rem(row32, 2) == b) & (row32 < 28)
            mean = jnp.sum(jnp.where(keep, line, 0.0), axis=0, keepdims=True) / 196.0
            pooled = jnp.where(lax.rem(row16, 4) == 2 * slot + b, mean, pooled)

    pltpu.make_async_copy(proj_hbm, proj, loc.at[3]).wait()
    weights = jnp.concatenate(
        [proj[pl.ds(pl.multiple_of(128 * a + 64 * c, 64), 64), :] for a in range(4)], axis=0
    )
    partial = jnp.dot(pooled.astype(BF16), weights, preferred_element_type=F32)
    part[0] = partial[:8]
    send(part.at[0], part.at[1], pt_s, pt_r, sibling)
    wait(part.at[1], pt_r)
    projected = part[0] + part[1]
    norm = jnp.sqrt(jnp.sum(projected * projected, axis=1, keepdims=True) + EPS)
    embed = (projected / norm).astype(BF16).astype(F32)

    row8 = lax.broadcasted_iota(jnp.int32, (8, 256), 0)
    zb[z] = jnp.where(row8 // 4 == lax.rem(z, 2), embed, 0.0)
    for k in range(1, N):
        send(zb.at[z], zb.at[z], d1_s, d1_r, zpeer[k])
    wait(zb.at[pl.ds(0, N - 1)], d1_r)
    yb[N - 1] = jnp.concatenate([zb[2 * k] + zb[2 * k + 1] for k in range(4)], axis=0).astype(BF16)
    for k in range(1, N):
        send(yb.at[N - 1], yb.at[k - 1], d2_s, d2_r, ypeer[k])
    wait(prs.at[pl.ds(0, 3)], pr_r)
    wait(yb.at[pl.ds(0, N - 1)], d2_r)

    images = yb[...].reshape(256, 256)
    for a in range(4):
        cols = pl.ds(SLICE * a, SLICE)
        e = jnp.exp(jnp.dot(images, prs[a], preferred_element_type=F32) / TEMP)
        ef[:, cols] = e
        hi = e.astype(BF16)
        ehi[:, cols] = hi
        elo[:, cols] = (e - hi.astype(F32)).astype(BF16)
        cb[0, N - 1, :, cols] = jnp.sum(e, axis=0, keepdims=True)

    for sweep in range(SINK):
        for k in range(1, N):
            send(cb.at[sweep, N - 1], cb.at[sweep, k - 1], c_s.at[sweep], c_r.at[sweep], xpeer[k])
        wait(cb.at[sweep, pl.ds(0, N - 1)], c_r.at[sweep])
        total = cb[sweep, 0]
        for k in range(1, N):
            total = total + cb[sweep, k]
        v = 1.0 / total
        if sweep == SINK - 1:
            break
        vv = split_rows(v)
        s = nt(vv, ehi[...]) + nt(vv, elo[...])
        rb[sweep, 0] = s[0:1] + s[1:2]
        send(rb.at[sweep, 0], rb.at[sweep, 1], r_s.at[sweep], r_r.at[sweep], sibling)
        wait(rb.at[sweep, 1], r_r.at[sweep])
        uu = split_rows(1.0 / (rb[sweep, 0] + rb[sweep, 1]))
        s = jnp.dot(uu, ehi[...], preferred_element_type=F32)
        s = s + jnp.dot(uu, elo[...], preferred_element_type=F32)
        cb[sweep + 1, N - 1] = s[0:1] + s[1:2]

    block = pl.ds(pl.multiple_of(32 * (N - 1) + 8 * (z // 2), 8), 8)
    fin[0] = ef[block, :] * v
    send(fin.at[0], fin.at[1], f_s, f_r, sibling)
    wait(fin.at[1], f_r)
    even = jnp.where(c == 0, fin[0], fin[1])
    odd = jnp.where(c == 0, fin[1], fin[0])
    rows = jnp.sum(even, axis=1, keepdims=True) + jnp.sum(odd, axis=1, keepdims=True)
    scale = PROTOS / rows
    even, odd = even * scale, odd * scale
    first = lax.rem(z, 2) * 4 + 2 * c
    rowc = lax.broadcasted_iota(jnp.int32, (8, SLICE), 0)
    for b in range(2):
        for a in range(4):
            for half, codes in ((0, even), (1, odd)):
                mine = jnp.where(rowc == first + b, codes[:, SLICE * a : SLICE * (a + 1)], 0.0)
                out_ref[pl.ds(b, 1), pl.ds(SLICE * (2 * a + half), SLICE)] = jnp.sum(
                    mine, axis=0, keepdims=True
                )

    wait(gath.at[pl.ds(0, 48), :], p1_s)
    wait(gath.at[pl.ds(0, 144), :], p2_s)
    wait(wide, sib_s)
    wait(prs.at[pl.ds(0, 3)], pr_s)
    wait(part.at[0], pt_s)
    wait(zb.at[pl.ds(0, N - 1)], d1_s)
    wait(yb.at[pl.ds(0, N - 1)], d2_s)
    for sweep in range(SINK):
        wait(cb.at[sweep, pl.ds(0, N - 1)], c_s.at[sweep])
    for sweep in range(SINK - 1):
        wait(rb.at[sweep, 0], r_s.at[sweep])
    wait(fin.at[0], f_s)


def shards(features, conv_weight, proj_weight, prototypes):
    maps = jnp.transpose(features[:, :, :, 0, :], (1, 2, 0, 3))
    maps = jnp.pad(maps, ((0, 0), (0, 2), (0, 0), (0, 0))).reshape(MAP, 512)
    weight = jnp.transpose(conv_weight[0])
    dma = pltpu.SemaphoreType.DMA
    return pl.pallas_call(
        kernel,
        out_shape=jax.ShapeDtypeStruct((2, PROTOS), F32),
        in_specs=[pl.BlockSpec(memory_space=pl.ANY)] * 4,
        out_specs=pl.BlockSpec(memory_space=pltpu.VMEM),
        scratch_shapes=[
            pltpu.VMEM((MAP, 512), BF16),
            pltpu.VMEM((MAP, 512), BF16),
            pltpu.VMEM((MAP + 96, 512), F32),
            pltpu.VMEM((2, 3, 512, 512), BF16),
            pltpu.VMEM((2, MAP, 256), F32),
            pltpu.VMEM((256, 4 * KQ), BF16),
            pltpu.VMEM((512, 256), BF16),
            pltpu.VMEM((256, SLICE), BF16),
            pltpu.VMEM((4, 256, SLICE), BF16),
            pltpu.VMEM((2, 8, 256), F32),
            pltpu.VMEM((N, 8, 256), F32),
            pltpu.VMEM((N, 32, 256), BF16),
            pltpu.VMEM((256, HALF), F32),
            pltpu.VMEM((256, HALF), BF16),
            pltpu.VMEM((256, HALF), BF16),
            pltpu.VMEM((SINK, N, 1, HALF), F32),
            pltpu.VMEM((SINK - 1, 2, 1, 256), F32),
            pltpu.VMEM((2, 8, HALF), F32),
            dma((4,)),
            dma, dma,
            dma, dma((3, 2)),
            dma, dma,
            dma, dma,
            dma, dma,
            dma, dma,
            dma, dma,
            dma((SINK,)), dma((SINK,)),
            dma((SINK - 1,)), dma((SINK - 1,)),
            dma, dma,
        ],
        compiler_params=pltpu.CompilerParams(
            collective_id=0, has_side_effects=True, vmem_limit_bytes=48 * 1024 * 1024
        ),
    )(maps, weight, proj_weight, prototypes)


def solution(mesh):
    return jax.shard_map(
        shards,
        mesh=mesh,
        in_specs=(
            P(("dp", "fsdp"), None, None, None, None),
            P(None, None, "fsdp"),
            P(),
            P(None, "fsdp"),
        ),
        out_specs=P(("dp", "fsdp"), None),
        check_vma=False,
    )
```

time: 487 us -> 75.3 us (0.15)
  blocking collectives: 339 us -> 0 us
  waiting for transfers between devices: 122 us -> 0 us
  Pallas kernels: 0 us -> 71.9 us
  between operations: 13.5 us -> 0.05 us
  matrix products: 7.98 us -> 0 us
    psum x3 -> x0, blocking collectives: 339 us -> none  [shards(): lax.psum(jnp.sum(probabilistic_cluster_share, axis=0), ('dp', 'fsdp'))]
    all_gather x2 -> x0, waiting for transfers between devices: 120 us -> none  [the longest x1 64.7 us: shards(): lax.all_gather(conv_weight, 'fsdp', axis=2, tiled=True)]
    pallas_call x0 -> x1, Pallas kernels: none -> 71.9 us  [shards(): pl.pallas_call(kernel, out_shape=jax.ShapeDtypeStruct((2, PROTOS), F32),...]
    dot_general x11 -> x0, matrix products: 7.98 us -> none  [the longest x9 7.3 us: conv_pool(): jnp.einsum('bhwgi,gio->bhwgo', window, tap_weights, preferred_element_typ...]
  transfers between devices with their start and end apart: 2 -> 0, of which waited for: 2 -> 0; matrix products, arithmetic and copies ran while one was open for 1% -> 0% of each run, Pallas kernels for 0% -> 0%
where the time goes in v1:
time: 75.3 us; the launch traced here: 75.1 us
  Pallas kernels  71.9 us (95%)
  local copies, waits for them, and re-layouts  3.16 us (4%)
    pallas_call x1, Pallas kernels, shards(): pl.pallas_call(kernel, out_shape=jax.ShapeDtypeStruct((2, PROTOS), F32),...  71.9 us
    unnamed x7, local copies, waits for them, and re-layouts  1.54 us

profile of v1, /device:TPU:1, one launch (start us, length us, event | category | flops | bytes accessed | tf_op | source)
XLA Modules:
  0.0 75.1 jit_solution(1375167660227415294)
XLA Ops:
  0.0 0.0 copy-start.2
  0.0 1.4 %pad.4 = bf16[14,16,2,512]{3,2,1,0:T(2,128)(2,1)S(1)} pad(bf16[14,14,2,512]{3,2,1,0:T(2,128)(2,1)} %bitcast.7, bf16[]{:T(256)} %constant.2.clone.1), padding=0_0x0_2x0_0x0_0 | pad | bytes 860162 | tf_op jit(solution)/shard_map/jit(_pad)/pad | solution.py:249
  1.5 0.0 copy-start
  1.5 0.0 copy-start.1
  1.5 0.2 reshape.3.x_hbm
  1.7 0.0 copy-done.2
  1.7 0.9 %copy-done = bf16[1,4608,64]{1,2,0:T(8,128)(2,1)S(1)} copy-done((bf16[1,4608,64]{1,2,0:T(8,128)(2,1)S(1)}, bf16[1,4608,64]{1,2,0:T(8,128)(2,1)}, u32[]{:S(2)}) %copy-start) | copy-done | bytes 589848
  2.5 0.1 copy-done.1
  2.6 71.9 %shard_map.46 = f32[2,3072]{1,0:T(2,128)S(1)} custom-call(bf16[448,512]{1,0:T(8,128)(2,1)S(1)} %reshape.3.x_hbm, bf16[64,4608]{1,0:T(8,128)(2,1)S(1)} %bitcast.6, bf16[512,256]{1,0:T(8,128)(2,1)S(1)} %copy-done.1, bf16[256,384]{1,0:T(8,128)(2,1)S(1)} %copy-done.2), custom_call_target="tpu_custom_call" | custom-call | tf_op jit(solution)/shard_map/pallas_call | solution.py:252
  74.5 0.6 copy.6
Async XLA Ops:
  0.0 1.7 %copy-start.2 = (bf16[256,384]{1,0:T(8,128)(2,1)S(1)}, bf16[256,384]{1,0:T(8,128)(2,1)}, u32[]{:S(2)}) copy-start(bf16[256,384]{1,0:T(8,128)(2,1)} %proto_hbm.1) | copy-start | bytes 589828
  1.5 1.1 %copy-start = (bf16[1,4608,64]{1,2,0:T(8,128)(2,1)S(1)}, bf16[1,4608,64]{1,2,0:T(8,128)(2,1)}, u32[]{:S(2)}) copy-start(bf16[1,4608,64]{1,2,0:T(8,128)(2,1)} %param.5) | copy-start | bytes 1769476
  1.5 1.1 %copy-start.1 = (bf16[512,256]{1,0:T(8,128)(2,1)S(1)}, bf16[512,256]{1,0:T(8,128)(2,1)}, u32[]{:S(2)}) copy-start(bf16[512,256]{1,0:T(8,128)(2,1)} %proj_hbm.1) | copy-start | bytes 786436

commit v2 on v1

--- a/solution.py
+++ b/solution.py
@@ -39,9 +39,9 @@
 
 def kernel(
     x_hbm, w_hbm, proj_hbm, proto_hbm, out_ref,
-    wide, sib, xf, xs, acc, gath, proj, proto, prs, part, zb, yb, ef, ehi, elo, cb, rb, fin,
+    wide, sib, xf, xs, acc, gath, proj, proto, prs, part, zb, yb, ef, eh, cb, rb, fin,
     loc, sib_s, sib_r, p1_s, p1_r, p2_s, p2_r, pr_s, pr_r, pt_s, pt_r,
-    d1_s, d1_r, d2_s, d2_r, c_s, c_r, r_s, r_r, f_s, f_r,
+    d1_s, d1_r, d2_s, d2_r, c_s, c_r, r_s, r_r, f_s, f_r, far,
 ):
     dp, fs = lax.axis_index("dp"), lax.axis_index("fsdp")
     x, y, zh = dp // 16, lax.rem(dp, 8), lax.rem(dp // 8, 2)
@@ -60,6 +60,12 @@
     def wait(ref, sem):
         pltpu.make_async_copy(ref, ref, sem).wait()
 
+    due = []
+
+    def drain():
+        for ref, sem in due + late:
+            wait(ref, sem)
+
     own = pl.ds(pl.multiple_of(zl * 64, 64), 64)
     for q in range(4):
         pltpu.make_async_copy(
@@ -69,18 +75,30 @@
     pltpu.make_async_copy(x_hbm, wide, loc.at[2]).start()
     pltpu.make_async_copy(proj_hbm, proj, loc.at[3]).start()
 
+    late = []
     barrier = pltpu.get_barrier_semaphore()
-    for to in [sibling] + zpeer[1:] + ypeer[1:] + xpeer[1:]:
+    near = [p[k] for p in (zpeer, xpeer, ypeer) for k in (1, 7, 2, 6)]
+    for to in [sibling] + near:
         pl.semaphore_signal(barrier, inc=1, device_id=to, device_id_type=MESH)
 
     pltpu.make_async_copy(proto_hbm, proto, loc.at[1]).wait()
     pw = proto[...].astype(F32)
     norm = jnp.sqrt(jnp.sum(pw * pw, axis=0, keepdims=True) + EPS)
     prs[zl] = (pw / norm).astype(BF16)
+
+    def spread(src, slot):
+        xf[...] = jnp.zeros((MAP + 96, 512), F32)
+        for h in range(14):
+            xf[pl.ds(48 + ROWS * h, 28), :] = src[h].astype(F32).reshape(28, 512)
+        for j in range(3):
+            xs[slot, j] = xf[pl.ds(14 + 2 * j, 512), :].astype(BF16)
+
     pltpu.make_async_copy(x_hbm, wide, loc.at[2]).wait()
+    spread(wide, c)
     wait(gath.at[pl.ds(0, 64), :], loc.at[0])
-
-    pl.semaphore_wait(barrier, 1 + 3 * (N - 1))
+    pltpu.make_async_copy(proj_hbm, proj, loc.at[3]).wait()
+
+    pl.semaphore_wait(barrier, 1 + len(near))
 
     color = [lax.rem(x + 2 * y, 4), lax.rem(2 * x + y, 4)]
 
@@ -100,15 +118,11 @@
             mine = piece(zl, h, g)
             send(mine, mine, p1_s, p1_r.at[1, h], zpeer[k])
     send(wide, sib, sib_s, sib_r, sibling)
-
-    def spread(src, slot):
-        xf[pl.ds(0, 48), :] = jnp.zeros((48, 512), F32)
-        xf[pl.ds(48, MAP), :] = src[...].astype(F32)
-        xf[pl.ds(48 + MAP, 48), :] = jnp.zeros((48, 512), F32)
-        for j in range(3):
-            xs[slot, j] = xf[pl.ds(14 + 2 * j, 512), :].astype(BF16)
-
-    spread(wide, c)
+    due.append((gath.at[pl.ds(0, 48), :], p1_s))
+    due.append((wide, sib_s))
+    late = [(sib, sib_r)]
+    for to in [p[k] for p in (zpeer, xpeer, ypeer) for k in (2, 6)]:
+        pl.semaphore_signal(far, inc=1, device_id=to, device_id_type=MESH)
 
     def forward(k, h):
         s = lax.rem(zl + k, 4)
@@ -119,17 +133,21 @@
         for g, to in ((0, part_[1]), (1, part_[7])):
             send(piece(s, h, g), piece(s, h, g), p2_s, p2_r, to)
 
-    for k in (1, 3, 2):
-        for h in range(2):
-            forward(k, h)
-
+    for k, h in ((1, 0), (3, 0), (1, 1), (3, 1), (2, 0), (2, 1)):
+        forward(k, h)
+
+    due.append((gath.at[pl.ds(0, 144), :], p2_s))
+    late.append((gath.at[pl.ds(0, 144), :], p2_r))
     for to in (zpeer[1], zpeer[7]):
         send(prs.at[zl], prs.at[zl], pr_s, pr_r, to)
     for g, to in ((0, zpeer[2]), (1, zpeer[6])):
         rows = pl.ds(128 * g, 128)
         send(prs.at[zl, rows], prs.at[zl, rows], pr_s, pr_r, to)
 
-    wait(sib, sib_r)
+    due.append((prs.at[pl.ds(0, 3)], pr_s))
+    late.append((prs.at[pl.ds(0, 3)], pr_r))
+    pl.semaphore_wait(far, 6)
+    wait(*late.pop(0))
     spread(sib, 1 - c)
 
     o = lax.broadcasted_iota(jnp.int32, (256, 512), 0)
@@ -138,7 +156,7 @@
     for slot in range(2):
         acc[slot] = nt(xs[slot, 1, pl.ds(32, MAP), :], pick)
 
-    wait(gath.at[pl.ds(0, 144), :], p2_r)
+    wait(*late.pop(0))
 
     def conv(slot, carry):
         for t in range(9):
@@ -158,27 +176,30 @@
             mean = jnp.sum(jnp.where(keep, line, 0.0), axis=0, keepdims=True) / 196.0
             pooled = jnp.where(lax.rem(row16, 4) == 2 * slot + b, mean, pooled)
 
-    pltpu.make_async_copy(proj_hbm, proj, loc.at[3]).wait()
     weights = jnp.concatenate(
         [proj[pl.ds(pl.multiple_of(128 * a + 64 * c, 64), 64), :] for a in range(4)], axis=0
     )
     partial = jnp.dot(pooled.astype(BF16), weights, preferred_element_type=F32)
     part[0] = partial[:8]
     send(part.at[0], part.at[1], pt_s, pt_r, sibling)
+    due.append((part.at[0], pt_s))
     wait(part.at[1], pt_r)
     projected = part[0] + part[1]
     norm = jnp.sqrt(jnp.sum(projected * projected, axis=1, keepdims=True) + EPS)
     embed = (projected / norm).astype(BF16).astype(F32)
 
     row8 = lax.broadcasted_iota(jnp.int32, (8, 256), 0)
-    zb[z] = jnp.where(row8 // 4 == lax.rem(z, 2), embed, 0.0)
+    zb[z] = jnp.where(row8 // 4 == lax.rem(z, 2), embed, 0.0).astype(BF16)
     for k in range(1, N):
         send(zb.at[z], zb.at[z], d1_s, d1_r, zpeer[k])
+    due.append((zb.at[pl.ds(0, N - 1)], d1_s))
     wait(zb.at[pl.ds(0, N - 1)], d1_r)
-    yb[N - 1] = jnp.concatenate([zb[2 * k] + zb[2 * k + 1] for k in range(4)], axis=0).astype(BF16)
+    pairs = [zb[2 * k].astype(F32) + zb[2 * k + 1].astype(F32) for k in range(4)]
+    yb[N - 1] = jnp.concatenate(pairs, axis=0).astype(BF16)
     for k in range(1, N):
         send(yb.at[N - 1], yb.at[k - 1], d2_s, d2_r, ypeer[k])
-    wait(prs.at[pl.ds(0, 3)], pr_r)
+    due.append((yb.at[pl.ds(0, N - 1)], d2_s))
+    wait(*late.pop(0))
     wait(yb.at[pl.ds(0, N - 1)], d2_r)
 
     images = yb[...].reshape(256, 256)
@@ -186,14 +207,13 @@
         cols = pl.ds(SLICE * a, SLICE)
         e = jnp.exp(jnp.dot(images, prs[a], preferred_element_type=F32) / TEMP)
         ef[:, cols] = e
-        hi = e.astype(BF16)
-        ehi[:, cols] = hi
-        elo[:, cols] = (e - hi.astype(F32)).astype(BF16)
+        eh[:, cols] = e.astype(BF16)
         cb[0, N - 1, :, cols] = jnp.sum(e, axis=0, keepdims=True)
 
     for sweep in range(SINK):
         for k in range(1, N):
             send(cb.at[sweep, N - 1], cb.at[sweep, k - 1], c_s.at[sweep], c_r.at[sweep], xpeer[k])
+        due.append((cb.at[sweep, pl.ds(0, N - 1)], c_s.at[sweep]))
         wait(cb.at[sweep, pl.ds(0, N - 1)], c_r.at[sweep])
         total = cb[sweep, 0]
         for k in range(1, N):
@@ -202,18 +222,19 @@
         if sweep == SINK - 1:
             break
         vv = split_rows(v)
-        s = nt(vv, ehi[...]) + nt(vv, elo[...])
+        s = nt(vv, eh[...])
         rb[sweep, 0] = s[0:1] + s[1:2]
         send(rb.at[sweep, 0], rb.at[sweep, 1], r_s.at[sweep], r_r.at[sweep], sibling)
+        due.append((rb.at[sweep, 0], r_s.at[sweep]))
         wait(rb.at[sweep, 1], r_r.at[sweep])
         uu = split_rows(1.0 / (rb[sweep, 0] + rb[sweep, 1]))
-        s = jnp.dot(uu, ehi[...], preferred_element_type=F32)
-        s = s + jnp.dot(uu, elo[...], preferred_element_type=F32)
+        s = jnp.dot(uu, eh[...], preferred_element_type=F32)
         cb[sweep + 1, N - 1] = s[0:1] + s[1:2]
 
     block = pl.ds(pl.multiple_of(32 * (N - 1) + 8 * (z // 2), 8), 8)
     fin[0] = ef[block, :] * v
     send(fin.at[0], fin.at[1], f_s, f_r, sibling)
+    due.append((fin.at[0], f_s))
     wait(fin.at[1], f_r)
     even = jnp.where(c == 0, fin[0], fin[1])
     odd = jnp.where(c == 0, fin[1], fin[0])
@@ -230,33 +251,21 @@
                     mine, axis=0, keepdims=True
                 )
 
-    wait(gath.at[pl.ds(0, 48), :], p1_s)
-    wait(gath.at[pl.ds(0, 144), :], p2_s)
-    wait(wide, sib_s)
-    wait(prs.at[pl.ds(0, 3)], pr_s)
-    wait(part.at[0], pt_s)
-    wait(zb.at[pl.ds(0, N - 1)], d1_s)
-    wait(yb.at[pl.ds(0, N - 1)], d2_s)
-    for sweep in range(SINK):
-        wait(cb.at[sweep, pl.ds(0, N - 1)], c_s.at[sweep])
-    for sweep in range(SINK - 1):
-        wait(rb.at[sweep, 0], r_s.at[sweep])
-    wait(fin.at[0], f_s)
+    drain()
 
 
 def shards(features, conv_weight, proj_weight, prototypes):
     maps = jnp.transpose(features[:, :, :, 0, :], (1, 2, 0, 3))
-    maps = jnp.pad(maps, ((0, 0), (0, 2), (0, 0), (0, 0))).reshape(MAP, 512)
     weight = jnp.transpose(conv_weight[0])
     dma = pltpu.SemaphoreType.DMA
     return pl.pallas_call(
         kernel,
         out_shape=jax.ShapeDtypeStruct((2, PROTOS), F32),
-        in_specs=[pl.BlockSpec(memory_space=pl.ANY)] * 4,
+        in_specs=[pl.BlockSpec(memory_space=pltpu.HBM)] * 4,
         out_specs=pl.BlockSpec(memory_space=pltpu.VMEM),
         scratch_shapes=[
-            pltpu.VMEM((MAP, 512), BF16),
-            pltpu.VMEM((MAP, 512), BF16),
+            pltpu.VMEM((14, 14, 2, 512), BF16),
+            pltpu.VMEM((14, 14, 2, 512), BF16),
             pltpu.VMEM((MAP + 96, 512), F32),
             pltpu.VMEM((2, 3, 512, 512), BF16),
             pltpu.VMEM((2, MAP, 256), F32),
@@ -265,10 +274,9 @@
             pltpu.VMEM((256, SLICE), BF16),
             pltpu.VMEM((4, 256, SLICE), BF16),
             pltpu.VMEM((2, 8, 256), F32),
-            pltpu.VMEM((N, 8, 256), F32),
+            pltpu.VMEM((N, 8, 256), BF16),
             pltpu.VMEM((N, 32, 256), BF16),
             pltpu.VMEM((256, HALF), F32),
-            pltpu.VMEM((256, HALF), BF16),
             pltpu.VMEM((256, HALF), BF16),
             pltpu.VMEM((SINK, N, 1, HALF), F32),
             pltpu.VMEM((SINK - 1, 2, 1, 256), F32),
@@ -284,11 +292,12 @@
             dma((SINK,)), dma((SINK,)),
             dma((SINK - 1,)), dma((SINK - 1,)),
             dma, dma,
+            pltpu.SemaphoreType.REGULAR,
         ],
         compiler_params=pltpu.CompilerParams(
-            collective_id=0, has_side_effects=True, vmem_limit_bytes=48 * 1024 * 1024
+            collective_id=0, has_side_effects=True, vmem_limit_bytes=48000 * 1024
         ),
-    )(maps, weight, proj_weight, prototypes)
+    )(*[pltpu.with_memory_space_constraint(a, pltpu.HBM) for a in (maps, weight, proj_weight, prototypes)])
 
 
 def solution(mesh):

time: 75.3 us -> 68.9 us (0.915)
  Pallas kernels: 71.9 us -> 68.1 us
  local copies, waits for them, and re-layouts: 3.16 us -> 0.61 us
    pallas_call x1, Pallas kernels: 71.9 us -> 68.1 us  [shards(): pl.pallas_call(kernel, out_shape=jax.ShapeDtypeStruct((2, PROTOS), F32),...]
    pad x1 -> x0, local copies, waits for them, and re-layouts: 1.44 us -> none  [shards(): maps = jnp.pad(maps, ((0, 0), (0, 2), (0, 0), (0, 0))).reshape(MAP, 512)]
    unnamed x7 -> x1, local copies, waits for them, and re-layouts: 1.54 us -> 0.61 us
where the time goes in v2:
time: 68.9 us; the launch traced here: 68.7 us
  Pallas kernels  68.1 us (99%)
    pallas_call x1, Pallas kernels, shards(): pl.pallas_call(kernel, out_shape=jax.ShapeDtypeStruct((2, PROTOS), F32),...  68.1 us

profile of v2, /device:TPU:1, one launch (start us, length us, event | category | flops | bytes accessed | tf_op | source)
XLA Modules:
  0.0 68.7 jit_solution(14778002747426785534)
XLA Ops:
  0.0 68.1 %shard_map.46 = f32[2,3072]{1,0:T(2,128)S(1)} custom-call(bf16[14,14,2,512]{3,2,1,0:T(2,128)(2,1)} %bitcast.7, bf16[64,4608]{1,0:T(8,128)(2,1)} %bitcast.6, bf16[512,256]{1,0:T(8,128)(2,1)} %proj_hbm.1, bf16[256,384]{1,0:T(8,128)(2,1)} %proto_hbm.1), custom_call_target="tpu_custom_call" | custom-call | tf_op jit(solution)/shard_map/pallas_call | solution.py:261
  68.1 0.6 copy.6

commit v3 on v2

--- a/solution.py
+++ b/solution.py
@@ -17,7 +17,7 @@
 N = 8
 ROWS = 32
 MAP = 14 * ROWS
-KQ = 1152
+STAGES = ((0, 640), (2560, 512))
 HALF = PROTOS // 2
 SLICE = 384
 
@@ -66,20 +66,17 @@
         for ref, sem in due + late:
             wait(ref, sem)
 
-    own = pl.ds(pl.multiple_of(zl * 64, 64), 64)
-    for q in range(4):
-        pltpu.make_async_copy(
-            w_hbm.at[:, pl.ds(q * KQ, KQ)], gath.at[own, pl.ds(q * KQ, KQ)], loc.at[0]
-        ).start()
-    pltpu.make_async_copy(proto_hbm, proto, loc.at[1]).start()
-    pltpu.make_async_copy(x_hbm, wide, loc.at[2]).start()
-    pltpu.make_async_copy(proj_hbm, proj, loc.at[3]).start()
-
     late = []
     barrier = pltpu.get_barrier_semaphore()
     near = [p[k] for p in (zpeer, xpeer, ypeer) for k in (1, 7, 2, 6)]
     for to in [sibling] + near:
         pl.semaphore_signal(barrier, inc=1, device_id=to, device_id_type=MESH)
+
+    own = pl.ds(pl.multiple_of(zl * 64, 64), 64)
+    pltpu.make_async_copy(w_hbm, gath.at[own], loc.at[0]).start()
+    pltpu.make_async_copy(proto_hbm, proto, loc.at[1]).start()
+    pltpu.make_async_copy(x_hbm, wide, loc.at[2]).start()
+    pltpu.make_async_copy(proj_hbm, proj, loc.at[3]).start()
 
     pltpu.make_async_copy(proto_hbm, proto, loc.at[1]).wait()
     pw = proto[...].astype(F32)
@@ -94,7 +91,6 @@
             xs[slot, j] = xf[pl.ds(14 + 2 * j, 512), :].astype(BF16)
 
     pltpu.make_async_copy(x_hbm, wide, loc.at[2]).wait()
-    spread(wide, c)
     wait(gath.at[pl.ds(0, 64), :], loc.at[0])
     pltpu.make_async_copy(proj_hbm, proj, loc.at[3]).wait()
 
@@ -102,21 +98,23 @@
 
     color = [lax.rem(x + 2 * y, 4), lax.rem(2 * x + y, 4)]
 
-    def piece(s, h, g=None):
+    def piece(stage, s, h, g=None):
+        first, size = STAGES[stage]
         row = s * 64 + h * 32
         rows = pl.ds(pl.multiple_of(row, 32), 32)
         if g is not None:
             rows = pl.ds(pl.multiple_of(row + 16 * g, 16), 16)
-        return gath.at[rows, pl.ds(pl.multiple_of(color[h] * KQ, 128), KQ)]
-
-    for h in range(2):
-        mine = piece(zl, h)
-        send(mine, mine, p1_s, p1_r.at[0, h], zpeer[7])
-        send(mine, mine, p1_s, p1_r.at[2, h], zpeer[1])
-    for h in range(2):
-        for g, k in ((0, 2), (1, 6)):
-            mine = piece(zl, h, g)
-            send(mine, mine, p1_s, p1_r.at[1, h], zpeer[k])
+        return gath.at[rows, pl.ds(pl.multiple_of(first + color[h] * size, 128), size)]
+
+    for stage in range(2):
+        for h in range(2):
+            mine = piece(stage, zl, h)
+            send(mine, mine, p1_s, p1_r.at[stage, 0, h], zpeer[7])
+            send(mine, mine, p1_s, p1_r.at[stage, 2, h], zpeer[1])
+        for h in range(2):
+            for g, k in ((0, 2), (1, 6)):
+                mine = piece(stage, zl, h, g)
+                send(mine, mine, p1_s, p1_r.at[stage, 1, h], zpeer[k])
     send(wide, sib, sib_s, sib_r, sibling)
     due.append((gath.at[pl.ds(0, 48), :], p1_s))
     due.append((wide, sib_s))
@@ -124,20 +122,25 @@
     for to in [p[k] for p in (zpeer, xpeer, ypeer) for k in (2, 6)]:
         pl.semaphore_signal(far, inc=1, device_id=to, device_id_type=MESH)
 
-    def forward(k, h):
+    spread(wide, c)
+
+    def forward(stage, k, h):
         s = lax.rem(zl + k, 4)
-        full, part_ = (xpeer, ypeer) if h == 0 else (ypeer, xpeer)
-        wait(piece(s, h), p1_r.at[k - 1, h])
+        full, half = (xpeer, ypeer) if h == 0 else (ypeer, xpeer)
+        whole = piece(stage, s, h)
+        wait(whole, p1_r.at[stage, k - 1, h])
         for to in (full[1], full[7]):
-            send(piece(s, h), piece(s, h), p2_s, p2_r, to)
-        for g, to in ((0, part_[1]), (1, part_[7])):
-            send(piece(s, h, g), piece(s, h, g), p2_s, p2_r, to)
-
-    for k, h in ((1, 0), (3, 0), (1, 1), (3, 1), (2, 0), (2, 1)):
-        forward(k, h)
-
+            send(whole, whole, p2_s, p2_r.at[stage], to)
+        for g, to in ((0, half[1]), (1, half[7])):
+            mine = piece(stage, s, h, g)
+            send(mine, mine, p2_s, p2_r.at[stage], to)
+
+    for stage in range(2):
+        for k, h in ((1, 0), (3, 0), (1, 1), (3, 1), (2, 0), (2, 1)):
+            forward(stage, k, h)
     due.append((gath.at[pl.ds(0, 144), :], p2_s))
-    late.append((gath.at[pl.ds(0, 144), :], p2_r))
+    late.append((gath.at[pl.ds(0, 80), :], p2_r.at[0]))
+    late.append((gath.at[pl.ds(0, 64), :], p2_r.at[1]))
     for to in (zpeer[1], zpeer[7]):
         send(prs.at[zl], prs.at[zl], pr_s, pr_r, to)
     for g, to in ((0, zpeer[2]), (1, zpeer[6])):
@@ -156,15 +159,19 @@
     for slot in range(2):
         acc[slot] = nt(xs[slot, 1, pl.ds(32, MAP), :], pick)
 
+    def conv(taps):
+        def maps(slot, carry):
+            for t in taps:
+                r, j = divmod(t, 3)
+                acc[slot] += nt(xs[slot, j, pl.ds(32 * r, MAP), :], gath[:, pl.ds(512 * t, 512)])
+            return carry
+
+        lax.fori_loop(0, 2, maps, 0)
+
     wait(*late.pop(0))
-
-    def conv(slot, carry):
-        for t in range(9):
-            r, j = divmod(t, 3)
-            acc[slot] += nt(xs[slot, j, pl.ds(32 * r, MAP), :], gath[:, pl.ds(512 * t, 512)])
-        return carry
-
-    lax.fori_loop(0, 2, conv, 0)
+    conv(range(5))
+    wait(*late.pop(0))
+    conv(range(5, 9))
 
     row32 = lax.broadcasted_iota(jnp.int32, (ROWS, 256), 0)
     row16 = lax.broadcasted_iota(jnp.int32, (16, 256), 0)
@@ -189,15 +196,15 @@
     embed = (projected / norm).astype(BF16).astype(F32)
 
     row8 = lax.broadcasted_iota(jnp.int32, (8, 256), 0)
-    zb[z] = jnp.where(row8 // 4 == lax.rem(z, 2), embed, 0.0).astype(BF16)
+    zb[y] = jnp.where(row8 // 4 == lax.rem(y, 2), embed, 0.0).astype(BF16)
     for k in range(1, N):
-        send(zb.at[z], zb.at[z], d1_s, d1_r, zpeer[k])
+        send(zb.at[y], zb.at[y], d1_s, d1_r, ypeer[k])
     due.append((zb.at[pl.ds(0, N - 1)], d1_s))
     wait(zb.at[pl.ds(0, N - 1)], d1_r)
     pairs = [zb[2 * k].astype(F32) + zb[2 * k + 1].astype(F32) for k in range(4)]
     yb[N - 1] = jnp.concatenate(pairs, axis=0).astype(BF16)
     for k in range(1, N):
-        send(yb.at[N - 1], yb.at[k - 1], d2_s, d2_r, ypeer[k])
+        send(yb.at[N - 1], yb.at[k - 1], d2_s, d2_r, zpeer[k])
     due.append((yb.at[pl.ds(0, N - 1)], d2_s))
     wait(*late.pop(0))
     wait(yb.at[pl.ds(0, N - 1)], d2_r)
@@ -231,7 +238,7 @@
         s = jnp.dot(uu, eh[...], preferred_element_type=F32)
         cb[sweep + 1, N - 1] = s[0:1] + s[1:2]
 
-    block = pl.ds(pl.multiple_of(32 * (N - 1) + 8 * (z // 2), 8), 8)
+    block = pl.ds(pl.multiple_of(32 * (N - 1) + 8 * (y // 2), 8), 8)
     fin[0] = ef[block, :] * v
     send(fin.at[0], fin.at[1], f_s, f_r, sibling)
     due.append((fin.at[0], f_s))
@@ -241,7 +248,7 @@
     rows = jnp.sum(even, axis=1, keepdims=True) + jnp.sum(odd, axis=1, keepdims=True)
     scale = PROTOS / rows
     even, odd = even * scale, odd * scale
-    first = lax.rem(z, 2) * 4 + 2 * c
+    first = lax.rem(y, 2) * 4 + 2 * c
     rowc = lax.broadcasted_iota(jnp.int32, (8, SLICE), 0)
     for b in range(2):
         for a in range(4):
@@ -269,7 +276,7 @@
             pltpu.VMEM((MAP + 96, 512), F32),
             pltpu.VMEM((2, 3, 512, 512), BF16),
             pltpu.VMEM((2, MAP, 256), F32),
-            pltpu.VMEM((256, 4 * KQ), BF16),
+            pltpu.VMEM((256, 4608), BF16),
             pltpu.VMEM((512, 256), BF16),
             pltpu.VMEM((256, SLICE), BF16),
             pltpu.VMEM((4, 256, SLICE), BF16),
@@ -283,8 +290,8 @@
             pltpu.VMEM((2, 8, HALF), F32),
             dma((4,)),
             dma, dma,
-            dma, dma((3, 2)),
-            dma, dma,
+            dma, dma((2, 3, 2)),
+            dma, dma((2,)),
             dma, dma,
             dma, dma,
             dma, dma,

time: 68.9 us -> 67.7 us (0.983)
  Pallas kernels: 68.1 us -> 67 us
    pallas_call x1, Pallas kernels: 68.1 us -> 67 us  [shards(): pl.pallas_call(kernel, out_shape=jax.ShapeDtypeStruct((2, PROTOS), F32),...]
where the time goes in v3:
time: 67.7 us; the launch traced here: 67.6 us
  Pallas kernels  67 us (99%)
    pallas_call x1, Pallas kernels, shards(): pl.pallas_call(kernel, out_shape=jax.ShapeDtypeStruct((2, PROTOS), F32),...  67 us

profile of v3, /device:TPU:1, one launch (start us, length us, event | category | flops | bytes accessed | tf_op | source)
XLA Modules:
  0.0 67.6 jit_solution(7779909049099765209)
XLA Ops:
  0.0 67.0 %shard_map.46 = f32[2,3072]{1,0:T(2,128)S(1)} custom-call(bf16[14,14,2,512]{3,2,1,0:T(2,128)(2,1)} %bitcast.7, bf16[64,4608]{1,0:T(8,128)(2,1)} %bitcast.6, bf16[512,256]{1,0:T(8,128)(2,1)} %proj_hbm.1, bf16[256,384]{1,0:T(8,128)(2,1)} %proto_hbm.1), custom_call_target="tpu_custom_call" | custom-call | tf_op jit(solution)/shard_map/pallas_call | solution.py:268
  67.0 0.6 copy.6

commit v4 on v3

--- a/solution.py
+++ b/solution.py
@@ -20,6 +20,8 @@
 STAGES = ((0, 640), (2560, 512))
 HALF = PROTOS // 2
 SLICE = 384
+GRID = 64
+CUBE = 8
 
 
 def device(x, y, z, c):
@@ -39,9 +41,9 @@
 
 def kernel(
     x_hbm, w_hbm, proj_hbm, proto_hbm, out_ref,
-    wide, sib, xf, xs, acc, gath, proj, proto, prs, part, zb, yb, ef, eh, cb, rb, fin,
+    wide, sib, xf, xs, acc, gath, proj, proto, prs, part, zb, ef, eh, cb, rb, fin,
     loc, sib_s, sib_r, p1_s, p1_r, p2_s, p2_r, pr_s, pr_r, pt_s, pt_r,
-    d1_s, d1_r, d2_s, d2_r, c_s, c_r, r_s, r_r, f_s, f_r, far,
+    d1_s, d1_r, c_s, c_r, r_s, r_r, f_s, f_r, far,
 ):
     dp, fs = lax.axis_index("dp"), lax.axis_index("fsdp")
     x, y, zh = dp // 16, lax.rem(dp, 8), lax.rem(dp // 8, 2)
@@ -51,6 +53,13 @@
     zpeer = [None] + [device(x, y, z + k, c) for k in range(1, N)]
     ypeer = [None] + [device(x, y + k, z, c) for k in range(1, N)]
     xpeer = [None] + [device(x + k, y, z, c) for k in range(1, N)]
+    steps = range(0, N, 2)
+    grid = [device(x + i, y + j, z + k, c) for i in steps for j in steps for k in steps][1:]
+    other = [a + 1 - 2 * lax.rem(a, 2) for a in (x, y, z)]
+    cube = []
+    for m in range(1, CUBE):
+        at = [b if m >> n & 1 else a for n, (a, b) in enumerate(zip((x, y, z), other))]
+        cube.append(device(*at, c))
 
     def send(src, dst, s, r, to):
         pltpu.make_async_remote_copy(
@@ -119,8 +128,8 @@
     due.append((gath.at[pl.ds(0, 48), :], p1_s))
     due.append((wide, sib_s))
     late = [(sib, sib_r)]
-    for to in [p[k] for p in (zpeer, xpeer, ypeer) for k in (2, 6)]:
-        pl.semaphore_signal(far, inc=1, device_id=to, device_id_type=MESH)
+    for to in near:
+        pl.semaphore_signal(far.at[0], inc=1, device_id=to, device_id_type=MESH)
 
     spread(wide, c)
 
@@ -138,6 +147,10 @@
     for stage in range(2):
         for k, h in ((1, 0), (3, 0), (1, 1), (3, 1), (2, 0), (2, 1)):
             forward(stage, k, h)
+        if stage == 0:
+            pl.semaphore_wait(far.at[0], len(near))
+            for to in (xpeer[2], xpeer[4], xpeer[6], cube[0]):
+                pl.semaphore_signal(far.at[1], inc=1, device_id=to, device_id_type=MESH)
     due.append((gath.at[pl.ds(0, 144), :], p2_s))
     late.append((gath.at[pl.ds(0, 80), :], p2_r.at[0]))
     late.append((gath.at[pl.ds(0, 64), :], p2_r.at[1]))
@@ -149,7 +162,6 @@
 
     due.append((prs.at[pl.ds(0, 3)], pr_s))
     late.append((prs.at[pl.ds(0, 3)], pr_r))
-    pl.semaphore_wait(far, 6)
     wait(*late.pop(0))
     spread(sib, 1 - c)
 
@@ -167,6 +179,10 @@
             return carry
 
         lax.fori_loop(0, 2, maps, 0)
+
+    pl.semaphore_wait(far.at[1], 4)
+    for to in (zpeer[2], zpeer[4], zpeer[6]):
+        pl.semaphore_signal(far.at[2], inc=1, device_id=to, device_id_type=MESH)
 
     wait(*late.pop(0))
     conv(range(5))
@@ -195,35 +211,28 @@
     norm = jnp.sqrt(jnp.sum(projected * projected, axis=1, keepdims=True) + EPS)
     embed = (projected / norm).astype(BF16).astype(F32)
 
-    row8 = lax.broadcasted_iota(jnp.int32, (8, 256), 0)
-    zb[y] = jnp.where(row8 // 4 == lax.rem(y, 2), embed, 0.0).astype(BF16)
-    for k in range(1, N):
-        send(zb.at[y], zb.at[y], d1_s, d1_r, ypeer[k])
-    due.append((zb.at[pl.ds(0, N - 1)], d1_s))
-    wait(zb.at[pl.ds(0, N - 1)], d1_r)
-    pairs = [zb[2 * k].astype(F32) + zb[2 * k + 1].astype(F32) for k in range(4)]
-    yb[N - 1] = jnp.concatenate(pairs, axis=0).astype(BF16)
-    for k in range(1, N):
-        send(yb.at[N - 1], yb.at[k - 1], d2_s, d2_r, zpeer[k])
-    due.append((yb.at[pl.ds(0, N - 1)], d2_s))
+    zb[0] = embed[:4].astype(BF16)
+    pl.semaphore_wait(far.at[2], 3)
+    for k, to in enumerate(grid):
+        send(zb.at[0], zb.at[k + 1], d1_s, d1_r, to)
+    due.append((zb.at[pl.ds(1, GRID - 1)], d1_s))
     wait(*late.pop(0))
-    wait(yb.at[pl.ds(0, N - 1)], d2_r)
-
-    images = yb[...].reshape(256, 256)
+    wait(zb.at[pl.ds(1, GRID - 1)], d1_r)
+    images = zb[...].astype(F32).reshape(256, 256).astype(BF16)
     for a in range(4):
         cols = pl.ds(SLICE * a, SLICE)
         e = jnp.exp(jnp.dot(images, prs[a], preferred_element_type=F32) / TEMP)
         ef[:, cols] = e
         eh[:, cols] = e.astype(BF16)
-        cb[0, N - 1, :, cols] = jnp.sum(e, axis=0, keepdims=True)
+        cb[0, CUBE - 1, :, cols] = jnp.sum(e, axis=0, keepdims=True)
 
     for sweep in range(SINK):
-        for k in range(1, N):
-            send(cb.at[sweep, N - 1], cb.at[sweep, k - 1], c_s.at[sweep], c_r.at[sweep], xpeer[k])
-        due.append((cb.at[sweep, pl.ds(0, N - 1)], c_s.at[sweep]))
-        wait(cb.at[sweep, pl.ds(0, N - 1)], c_r.at[sweep])
+        for k, to in enumerate(cube):
+            send(cb.at[sweep, CUBE - 1], cb.at[sweep, k], c_s.at[sweep], c_r.at[sweep], to)
+        due.append((cb.at[sweep, pl.ds(0, CUBE - 1)], c_s.at[sweep]))
+        wait(cb.at[sweep, pl.ds(0, CUBE - 1)], c_r.at[sweep])
         total = cb[sweep, 0]
-        for k in range(1, N):
+        for k in range(1, CUBE):
             total = total + cb[sweep, k]
         v = 1.0 / total
         if sweep == SINK - 1:
@@ -236,10 +245,9 @@
         wait(rb.at[sweep, 1], r_r.at[sweep])
         uu = split_rows(1.0 / (rb[sweep, 0] + rb[sweep, 1]))
         s = jnp.dot(uu, eh[...], preferred_element_type=F32)
-        cb[sweep + 1, N - 1] = s[0:1] + s[1:2]
-
-    block = pl.ds(pl.multiple_of(32 * (N - 1) + 8 * (y // 2), 8), 8)
-    fin[0] = ef[block, :] * v
+        cb[sweep + 1, CUBE - 1] = s[0:1] + s[1:2]
+
+    fin[0] = ef[pl.ds(0, 8), :] * v
     send(fin.at[0], fin.at[1], f_s, f_r, sibling)
     due.append((fin.at[0], f_s))
     wait(fin.at[1], f_r)
@@ -248,7 +256,7 @@
     rows = jnp.sum(even, axis=1, keepdims=True) + jnp.sum(odd, axis=1, keepdims=True)
     scale = PROTOS / rows
     even, odd = even * scale, odd * scale
-    first = lax.rem(y, 2) * 4 + 2 * c
+    first = 2 * c
     rowc = lax.broadcasted_iota(jnp.int32, (8, SLICE), 0)
     for b in range(2):
         for a in range(4):
@@ -281,11 +289,10 @@
             pltpu.VMEM((256, SLICE), BF16),
             pltpu.VMEM((4, 256, SLICE), BF16),
             pltpu.VMEM((2, 8, 256), F32),
-            pltpu.VMEM((N, 8, 256), BF16),
-            pltpu.VMEM((N, 32, 256), BF16),
+            pltpu.VMEM((GRID, 4, 256), BF16),
             pltpu.VMEM((256, HALF), F32),
             pltpu.VMEM((256, HALF), BF16),
-            pltpu.VMEM((SINK, N, 1, HALF), F32),
+            pltpu.VMEM((SINK, CUBE, 1, HALF), F32),
             pltpu.VMEM((SINK - 1, 2, 1, 256), F32),
             pltpu.VMEM((2, 8, HALF), F32),
             dma((4,)),
@@ -295,11 +302,10 @@
             dma, dma,
             dma, dma,
             dma, dma,
-            dma, dma,
             dma((SINK,)), dma((SINK,)),
             dma((SINK - 1,)), dma((SINK - 1,)),
             dma, dma,
-            pltpu.SemaphoreType.REGULAR,
+            pltpu.SemaphoreType.REGULAR((3,)),
         ],
         compiler_params=pltpu.CompilerParams(
             collective_id=0, has_side_effects=True, vmem_limit_bytes=48000 * 1024

time: 67.7 us -> 64.1 us (0.947)
  Pallas kernels: 67 us -> 63.3 us
    pallas_call x1, Pallas kernels: 67 us -> 63.3 us  [shards(): pl.pallas_call(kernel, out_shape=jax.ShapeDtypeStruct((2, PROTOS), F32),...]
where the time goes in v4:
time: 64.1 us; the launch traced here: 63.9 us
  Pallas kernels  63.3 us (99%)
    pallas_call x1, Pallas kernels, shards(): pl.pallas_call(kernel, out_shape=jax.ShapeDtypeStruct((2, PROTOS), F32),...  63.3 us

profile of v4, /device:TPU:1, one launch (start us, length us, event | category | flops | bytes accessed | tf_op | source)
XLA Modules:
  0.0 63.9 jit_solution(653600384895377724)
XLA Ops:
  0.0 63.3 %shard_map.46 = f32[2,3072]{1,0:T(2,128)S(1)} custom-call(bf16[14,14,2,512]{3,2,1,0:T(2,128)(2,1)} %bitcast.7, bf16[64,4608]{1,0:T(8,128)(2,1)} %bitcast.6, bf16[512,256]{1,0:T(8,128)(2,1)} %proj_hbm.1, bf16[256,384]{1,0:T(8,128)(2,1)} %proto_hbm.1), custom_call_target="tpu_custom_call" | custom-call | tf_op jit(solution)/shard_map/pallas_call | solution.py:276
  63.3 0.6 copy.6

commit v5 on v4

--- a/solution.py
+++ b/solution.py
@@ -42,7 +42,7 @@
 def kernel(
     x_hbm, w_hbm, proj_hbm, proto_hbm, out_ref,
     wide, sib, xf, xs, acc, gath, proj, proto, prs, part, zb, ef, eh, cb, rb, fin,
-    loc, sib_s, sib_r, p1_s, p1_r, p2_s, p2_r, pr_s, pr_r, pt_s, pt_r,
+    loc, sib_s, sib_r, p1_s, p1_r, p2_s, p2_r, p3_s, pr_s, pr_r, pt_s, pt_r,
     d1_s, d1_r, c_s, c_r, r_s, r_r, f_s, f_r, far,
 ):
     dp, fs = lax.axis_index("dp"), lax.axis_index("fsdp")
@@ -54,10 +54,12 @@
     ypeer = [None] + [device(x, y + k, z, c) for k in range(1, N)]
     xpeer = [None] + [device(x + k, y, z, c) for k in range(1, N)]
     steps = range(0, N, 2)
-    grid = [device(x + i, y + j, z + k, c) for i in steps for j in steps for k in steps][1:]
+    grid = [(i, j, k) for i in steps for j in steps for k in steps][1:]
+    grid.sort(key=lambda step: -sum(min(a, N - a) for a in step))
+    grid = [device(x + i, y + j, z + k, c) for i, j, k in grid]
     other = [a + 1 - 2 * lax.rem(a, 2) for a in (x, y, z)]
     cube = []
-    for m in range(1, CUBE):
+    for m in (7, 6, 5, 3, 4, 2, 1):
         at = [b if m >> n & 1 else a for n, (a, b) in enumerate(zip((x, y, z), other))]
         cube.append(device(*at, c))
 
@@ -107,13 +109,14 @@
 
     color = [lax.rem(x + 2 * y, 4), lax.rem(2 * x + y, 4)]
 
-    def piece(stage, s, h, g=None):
+    def piece(stage, s, h, g=None, ahead=0):
         first, size = STAGES[stage]
+        hue = lax.rem(color[h] + ahead, 4)
         row = s * 64 + h * 32
         rows = pl.ds(pl.multiple_of(row, 32), 32)
         if g is not None:
             rows = pl.ds(pl.multiple_of(row + 16 * g, 16), 16)
-        return gath.at[rows, pl.ds(pl.multiple_of(first + color[h] * size, 128), size)]
+        return gath.at[rows, pl.ds(pl.multiple_of(first + hue * size, 128), size)]
 
     for stage in range(2):
         for h in range(2):
@@ -124,6 +127,13 @@
             for g, k in ((0, 2), (1, 6)):
                 mine = piece(stage, zl, h, g)
                 send(mine, mine, p1_s, p1_r.at[stage, 1, h], zpeer[k])
+    for h in range(2):
+        mine = piece(1, zl, h, ahead=2)
+        send(mine, mine, p3_s, p2_r.at[1], zpeer[7])
+        send(mine, mine, p3_s, p2_r.at[1], zpeer[1])
+        for g, k in ((0, 2), (1, 6)):
+            mine = piece(1, zl, h, g, ahead=2)
+            send(mine, mine, p3_s, p2_r.at[1], zpeer[k])
     send(wide, sib, sib_s, sib_r, sibling)
     due.append((gath.at[pl.ds(0, 48), :], p1_s))
     due.append((wide, sib_s))
@@ -139,19 +149,22 @@
         whole = piece(stage, s, h)
         wait(whole, p1_r.at[stage, k - 1, h])
         for to in (full[1], full[7]):
-            send(whole, whole, p2_s, p2_r.at[stage], to)
-        for g, to in ((0, half[1]), (1, half[7])):
-            mine = piece(stage, s, h, g)
-            send(mine, mine, p2_s, p2_r.at[stage], to)
+            send(whole, whole, p2_s.at[stage], p2_r.at[stage], to)
+        if stage == 0:
+            for g, to in ((0, half[1]), (1, half[7])):
+                mine = piece(stage, s, h, g)
+                send(mine, mine, p2_s.at[stage], p2_r.at[stage], to)
 
     for stage in range(2):
         for k, h in ((1, 0), (3, 0), (1, 1), (3, 1), (2, 0), (2, 1)):
             forward(stage, k, h)
         if stage == 0:
             pl.semaphore_wait(far.at[0], len(near))
-            for to in (xpeer[2], xpeer[4], xpeer[6], cube[0]):
+            for to in (xpeer[2], xpeer[4], xpeer[6], cube[6]):
                 pl.semaphore_signal(far.at[1], inc=1, device_id=to, device_id_type=MESH)
-    due.append((gath.at[pl.ds(0, 144), :], p2_s))
+    due.append((gath.at[pl.ds(0, 80), :], p2_s.at[0]))
+    due.append((gath.at[:, pl.ds(0, 768)], p2_s.at[1]))
+    due.append((gath.at[pl.ds(0, 192), pl.ds(0, 512)], p3_s))
     late.append((gath.at[pl.ds(0, 80), :], p2_r.at[0]))
     late.append((gath.at[pl.ds(0, 64), :], p2_r.at[1]))
     for to in (zpeer[1], zpeer[7]):
@@ -247,7 +260,7 @@
         s = jnp.dot(uu, eh[...], preferred_element_type=F32)
         cb[sweep + 1, CUBE - 1] = s[0:1] + s[1:2]
 
-    fin[0] = ef[pl.ds(0, 8), :] * v
+    fin[0] = ef[pl.ds(0, 8), :][:4] * v
     send(fin.at[0], fin.at[1], f_s, f_r, sibling)
     due.append((fin.at[0], f_s))
     wait(fin.at[1], f_r)
@@ -257,7 +270,7 @@
     scale = PROTOS / rows
     even, odd = even * scale, odd * scale
     first = 2 * c
-    rowc = lax.broadcasted_iota(jnp.int32, (8, SLICE), 0)
+    rowc = lax.broadcasted_iota(jnp.int32, (4, SLICE), 0)
     for b in range(2):
         for a in range(4):
             for half, codes in ((0, even), (1, odd)):
@@ -294,11 +307,11 @@
             pltpu.VMEM((256, HALF), BF16),
             pltpu.VMEM((SINK, CUBE, 1, HALF), F32),
             pltpu.VMEM((SINK - 1, 2, 1, 256), F32),
-            pltpu.VMEM((2, 8, HALF), F32),
+            pltpu.VMEM((2, 4, HALF), F32),
             dma((4,)),
             dma, dma,
             dma, dma((2, 3, 2)),
-            dma, dma((2,)),
+            dma((2,)), dma((2,)), dma,
             dma, dma,
             dma, dma,
             dma, dma,

time: 64.1 us -> 63.2 us (0.986)
  Pallas kernels: 63.3 us -> 62.4 us
    pallas_call x1, Pallas kernels: 63.3 us -> 62.4 us  [shards(): pl.pallas_call(kernel, out_shape=jax.ShapeDtypeStruct((2, PROTOS), F32),...]
where the time goes in v5:
time: 63.2 us; the launch traced here: 63 us
  Pallas kernels  62.4 us (99%)
    pallas_call x1, Pallas kernels, shards(): pl.pallas_call(kernel, out_shape=jax.ShapeDtypeStruct((2, PROTOS), F32),...  62.4 us

profile of v5, /device:TPU:1, one launch (start us, length us, event | category | flops | bytes accessed | tf_op | source)
XLA Modules:
  0.0 63.0 jit_solution(16688393575337842620)
XLA Ops:
  0.0 62.4 %shard_map.46 = f32[2,3072]{1,0:T(2,128)S(1)} custom-call(bf16[14,14,2,512]{3,2,1,0:T(2,128)(2,1)} %bitcast.7, bf16[64,4608]{1,0:T(8,128)(2,1)} %bitcast.6, bf16[512,256]{1,0:T(8,128)(2,1)} %proj_hbm.1, bf16[256,384]{1,0:T(8,128)(2,1)} %proto_hbm.1), custom_call_target="tpu_custom_call" | custom-call | tf_op jit(solution)/shard_map/pallas_call | solution.py:289
  62.4 0.6 copy.6

commit v6 on v5

--- a/solution.py
+++ b/solution.py
@@ -17,7 +17,8 @@
 N = 8
 ROWS = 32
 MAP = 14 * ROWS
-STAGES = ((0, 640), (2560, 512))
+STAGES = ((0, 512), (2048, 384), (3584, 256))
+DIRECT = 1
 HALF = PROTOS // 2
 SLICE = 384
 GRID = 64
@@ -58,10 +59,11 @@
     grid.sort(key=lambda step: -sum(min(a, N - a) for a in step))
     grid = [device(x + i, y + j, z + k, c) for i, j, k in grid]
     other = [a + 1 - 2 * lax.rem(a, 2) for a in (x, y, z)]
-    cube = []
+    cube, cross = [], []
     for m in (7, 6, 5, 3, 4, 2, 1):
         at = [b if m >> n & 1 else a for n, (a, b) in enumerate(zip((x, y, z), other))]
         cube.append(device(*at, c))
+        cross.append(device(*at, c + 1))
 
     def send(src, dst, s, r, to):
         pltpu.make_async_remote_copy(
@@ -118,7 +120,7 @@
             rows = pl.ds(pl.multiple_of(row + 16 * g, 16), 16)
         return gath.at[rows, pl.ds(pl.multiple_of(first + hue * size, 128), size)]
 
-    for stage in range(2):
+    for stage in range(3):
         for h in range(2):
             mine = piece(stage, zl, h)
             send(mine, mine, p1_s, p1_r.at[stage, 0, h], zpeer[7])
@@ -128,12 +130,12 @@
                 mine = piece(stage, zl, h, g)
                 send(mine, mine, p1_s, p1_r.at[stage, 1, h], zpeer[k])
     for h in range(2):
-        mine = piece(1, zl, h, ahead=2)
-        send(mine, mine, p3_s, p2_r.at[1], zpeer[7])
-        send(mine, mine, p3_s, p2_r.at[1], zpeer[1])
+        mine = piece(DIRECT, zl, h, ahead=2)
+        send(mine, mine, p3_s, p2_r.at[DIRECT], zpeer[7])
+        send(mine, mine, p3_s, p2_r.at[DIRECT], zpeer[1])
         for g, k in ((0, 2), (1, 6)):
-            mine = piece(1, zl, h, g, ahead=2)
-            send(mine, mine, p3_s, p2_r.at[1], zpeer[k])
+            mine = piece(DIRECT, zl, h, g, ahead=2)
+            send(mine, mine, p3_s, p2_r.at[DIRECT], zpeer[k])
     send(wide, sib, sib_s, sib_r, sibling)
     due.append((gath.at[pl.ds(0, 48), :], p1_s))
     due.append((wide, sib_s))
@@ -150,23 +152,22 @@
         wait(whole, p1_r.at[stage, k - 1, h])
         for to in (full[1], full[7]):
             send(whole, whole, p2_s.at[stage], p2_r.at[stage], to)
-        if stage == 0:
+        if stage != DIRECT:
             for g, to in ((0, half[1]), (1, half[7])):
                 mine = piece(stage, s, h, g)
                 send(mine, mine, p2_s.at[stage], p2_r.at[stage], to)
 
-    for stage in range(2):
+    for stage in range(3):
         for k, h in ((1, 0), (3, 0), (1, 1), (3, 1), (2, 0), (2, 1)):
             forward(stage, k, h)
         if stage == 0:
             pl.semaphore_wait(far.at[0], len(near))
             for to in (xpeer[2], xpeer[4], xpeer[6], cube[6]):
                 pl.semaphore_signal(far.at[1], inc=1, device_id=to, device_id_type=MESH)
-    due.append((gath.at[pl.ds(0, 80), :], p2_s.at[0]))
-    due.append((gath.at[:, pl.ds(0, 768)], p2_s.at[1]))
-    due.append((gath.at[pl.ds(0, 192), pl.ds(0, 512)], p3_s))
-    late.append((gath.at[pl.ds(0, 80), :], p2_r.at[0]))
-    late.append((gath.at[pl.ds(0, 64), :], p2_r.at[1]))
+    for stage, (sent, came) in enumerate(((64, 64), (32, 48), (32, 32))):
+        due.append((gath.at[pl.ds(0, sent), :], p2_s.at[stage]))
+        late.append((gath.at[pl.ds(0, came), :], p2_r.at[stage]))
+    due.append((gath.at[pl.ds(0, 16), :], p3_s))
     for to in (zpeer[1], zpeer[7]):
         send(prs.at[zl], prs.at[zl], pr_s, pr_r, to)
     for g, to in ((0, zpeer[2]), (1, zpeer[6])):
@@ -184,23 +185,19 @@
     for slot in range(2):
         acc[slot] = nt(xs[slot, 1, pl.ds(32, MAP), :], pick)
 
-    def conv(taps):
-        def maps(slot, carry):
+    pl.semaphore_wait(far.at[1], 4)
+    for to in (zpeer[2], zpeer[4], zpeer[6], sibling):
+        pl.semaphore_signal(far.at[2], inc=1, device_id=to, device_id_type=MESH)
+
+    for taps in (range(4), range(4, 7), range(7, 9)):
+        wait(*late.pop(0))
+        for slot in range(2):
+            total = acc[slot]
             for t in taps:
                 r, j = divmod(t, 3)
-                acc[slot] += nt(xs[slot, j, pl.ds(32 * r, MAP), :], gath[:, pl.ds(512 * t, 512)])
-            return carry
-
-        lax.fori_loop(0, 2, maps, 0)
-
-    pl.semaphore_wait(far.at[1], 4)
-    for to in (zpeer[2], zpeer[4], zpeer[6]):
-        pl.semaphore_signal(far.at[2], inc=1, device_id=to, device_id_type=MESH)
-
-    wait(*late.pop(0))
-    conv(range(5))
-    wait(*late.pop(0))
-    conv(range(5, 9))
+                maps = xs[slot, j, pl.ds(32 * r, MAP), :]
+                total = total + nt(maps, gath[:, pl.ds(512 * t, 512)])
+            acc[slot] = total
 
     row32 = lax.broadcasted_iota(jnp.int32, (ROWS, 256), 0)
     row16 = lax.broadcasted_iota(jnp.int32, (16, 256), 0)
@@ -225,7 +222,7 @@
     embed = (projected / norm).astype(BF16).astype(F32)
 
     zb[0] = embed[:4].astype(BF16)
-    pl.semaphore_wait(far.at[2], 3)
+    pl.semaphore_wait(far.at[2], 4)
     for k, to in enumerate(grid):
         send(zb.at[0], zb.at[k + 1], d1_s, d1_r, to)
     due.append((zb.at[pl.ds(1, GRID - 1)], d1_s))
@@ -239,17 +236,23 @@
         eh[:, cols] = e.astype(BF16)
         cb[0, CUBE - 1, :, cols] = jnp.sum(e, axis=0, keepdims=True)
 
-    for sweep in range(SINK):
+    def total_of(sums):
+        total = sums[0]
+        for k in range(1, CUBE):
+            total = total + sums[k]
+        return total
+
+    for sweep in range(SINK - 1):
+        sums = cb.at[sweep]
         for k, to in enumerate(cube):
-            send(cb.at[sweep, CUBE - 1], cb.at[sweep, k], c_s.at[sweep], c_r.at[sweep], to)
-        due.append((cb.at[sweep, pl.ds(0, CUBE - 1)], c_s.at[sweep]))
-        wait(cb.at[sweep, pl.ds(0, CUBE - 1)], c_r.at[sweep])
-        total = cb[sweep, 0]
-        for k in range(1, CUBE):
-            total = total + cb[sweep, k]
-        v = 1.0 / total
-        if sweep == SINK - 1:
-            break
+            send(sums.at[CUBE - 1], sums.at[k], c_s.at[sweep], c_r.at[sweep], to)
+        due.append((sums.at[pl.ds(0, CUBE - 1)], c_s.at[sweep]))
+        if sweep == 0:
+            fin[0] = ef[pl.ds(0, 8), :][:4]
+            send(fin.at[0], fin.at[1], f_s, f_r, sibling)
+            due.append((fin.at[0], f_s))
+        wait(sums.at[pl.ds(0, CUBE - 1)], c_r.at[sweep])
+        v = 1.0 / total_of(sums)
         vv = split_rows(v)
         s = nt(vv, eh[...])
         rb[sweep, 0] = s[0:1] + s[1:2]
@@ -260,12 +263,20 @@
         s = jnp.dot(uu, eh[...], preferred_element_type=F32)
         cb[sweep + 1, CUBE - 1] = s[0:1] + s[1:2]
 
-    fin[0] = ef[pl.ds(0, 8), :][:4] * v
-    send(fin.at[0], fin.at[1], f_s, f_r, sibling)
-    due.append((fin.at[0], f_s))
+    sums, theirs = cb.at[2], cb.at[3]
+    for k in range(CUBE - 1):
+        send(sums.at[CUBE - 1], sums.at[k], c_s.at[2], c_r.at[2], cube[k])
+        send(sums.at[CUBE - 1], theirs.at[k], c_s.at[3], c_r.at[3], cross[k])
+    send(sums.at[CUBE - 1], theirs.at[CUBE - 1], c_s.at[3], c_r.at[3], sibling)
+    due.append((sums.at[pl.ds(0, CUBE - 1)], c_s.at[2]))
+    due.append((theirs, c_s.at[3]))
     wait(fin.at[1], f_r)
-    even = jnp.where(c == 0, fin[0], fin[1])
-    odd = jnp.where(c == 0, fin[1], fin[0])
+    wait(sums.at[pl.ds(0, CUBE - 1)], c_r.at[2])
+    wait(theirs, c_r.at[3])
+    here = fin[0] * (1.0 / total_of(sums))
+    there = fin[1] * (1.0 / total_of(theirs))
+    even = jnp.where(c == 0, here, there)
+    odd = jnp.where(c == 0, there, here)
     rows = jnp.sum(even, axis=1, keepdims=True) + jnp.sum(odd, axis=1, keepdims=True)
     scale = PROTOS / rows
     even, odd = even * scale, odd * scale
@@ -305,17 +316,17 @@
             pltpu.VMEM((GRID, 4, 256), BF16),
             pltpu.VMEM((256, HALF), F32),
             pltpu.VMEM((256, HALF), BF16),
-            pltpu.VMEM((SINK, CUBE, 1, HALF), F32),
+            pltpu.VMEM((SINK + 1, CUBE, 1, HALF), F32),
             pltpu.VMEM((SINK - 1, 2, 1, 256), F32),
             pltpu.VMEM((2, 4, HALF), F32),
             dma((4,)),
             dma, dma,
-            dma, dma((2, 3, 2)),
-            dma((2,)), dma((2,)), dma,
-            dma, dma,
-            dma, dma,
-            dma, dma,
-            dma((SINK,)), dma((SINK,)),
+            dma, dma((3, 3, 2)),
+            dma((3,)), dma((3,)), dma,
+            dma, dma,
+            dma, dma,
+            dma, dma,
+            dma((SINK + 1,)), dma((SINK + 1,)),
             dma((SINK - 1,)), dma((SINK - 1,)),
             dma, dma,
             pltpu.SemaphoreType.REGULAR((3,)),

time: 63.2 us -> 61.5 us (0.973)
  Pallas kernels: 62.4 us -> 60.7 us
    pallas_call x1, Pallas kernels: 62.4 us -> 60.7 us  [shards(): pl.pallas_call(kernel, out_shape=jax.ShapeDtypeStruct((2, PROTOS), F32),...]
where the time goes in v6:
time: 61.5 us; the launch traced here: 61.4 us
  Pallas kernels  60.7 us (99%)
    pallas_call x1, Pallas kernels, shards(): pl.pallas_call(kernel, out_shape=jax.ShapeDtypeStruct((2, PROTOS), F32),...  60.7 us

profile of v6, /device:TPU:1, one launch (start us, length us, event | category | flops | bytes accessed | tf_op | source)
XLA Modules:
  0.0 61.4 jit_solution(2661536610246430136)
XLA Ops:
  0.0 60.7 %shard_map.46 = f32[2,3072]{1,0:T(2,128)S(1)} custom-call(bf16[14,14,2,512]{3,2,1,0:T(2,128)(2,1)} %bitcast.7, bf16[64,4608]{1,0:T(8,128)(2,1)} %bitcast.6, bf16[512,256]{1,0:T(8,128)(2,1)} %proj_hbm.1, bf16[256,384]{1,0:T(8,128)(2,1)} %proto_hbm.1), custom_call_target="tpu_custom_call" | custom-call | tf_op jit(solution)/shard_map/pallas_call | solution.py:300
  60.8 0.6 copy.6

commit v7 on v6

--- a/solution.py
+++ b/solution.py
@@ -81,7 +81,7 @@
 
     late = []
     barrier = pltpu.get_barrier_semaphore()
-    near = [p[k] for p in (zpeer, xpeer, ypeer) for k in (1, 7, 2, 6)]
+    near = [p[k] for ks in ((2, 6), (1, 7)) for p in (zpeer, xpeer, ypeer) for k in ks]
     for to in [sibling] + near:
         pl.semaphore_signal(barrier, inc=1, device_id=to, device_id_type=MESH)
 
@@ -157,8 +157,17 @@
                 mine = piece(stage, s, h, g)
                 send(mine, mine, p2_s.at[stage], p2_r.at[stage], to)
 
+    def prototypes():
+        for to in (zpeer[1], zpeer[7]):
+            send(prs.at[zl], prs.at[zl], pr_s, pr_r, to)
+        for g, to in ((0, zpeer[2]), (1, zpeer[6])):
+            rows = pl.ds(128 * g, 128)
+            send(prs.at[zl, rows], prs.at[zl, rows], pr_s, pr_r, to)
+
     for stage in range(3):
         for k, h in ((1, 0), (3, 0), (1, 1), (3, 1), (2, 0), (2, 1)):
+            if stage == 2 and (k, h) == (2, 0):
+                prototypes()
             forward(stage, k, h)
         if stage == 0:
             pl.semaphore_wait(far.at[0], len(near))
@@ -168,12 +177,6 @@
         due.append((gath.at[pl.ds(0, sent), :], p2_s.at[stage]))
         late.append((gath.at[pl.ds(0, came), :], p2_r.at[stage]))
     due.append((gath.at[pl.ds(0, 16), :], p3_s))
-    for to in (zpeer[1], zpeer[7]):
-        send(prs.at[zl], prs.at[zl], pr_s, pr_r, to)
-    for g, to in ((0, zpeer[2]), (1, zpeer[6])):
-        rows = pl.ds(128 * g, 128)
-        send(prs.at[zl, rows], prs.at[zl, rows], pr_s, pr_r, to)
-
     due.append((prs.at[pl.ds(0, 3)], pr_s))
     late.append((prs.at[pl.ds(0, 3)], pr_r))
     wait(*late.pop(0))
@@ -224,17 +227,25 @@
     zb[0] = embed[:4].astype(BF16)
     pl.semaphore_wait(far.at[2], 4)
     for k, to in enumerate(grid):
-        send(zb.at[0], zb.at[k + 1], d1_s, d1_r, to)
+        send(zb.at[0], zb.at[k + 1], d1_s, d1_r.at[(k + 1) // 32], to)
     due.append((zb.at[pl.ds(1, GRID - 1)], d1_s))
     wait(*late.pop(0))
-    wait(zb.at[pl.ds(1, GRID - 1)], d1_r)
-    images = zb[...].astype(F32).reshape(256, 256).astype(BF16)
-    for a in range(4):
-        cols = pl.ds(SLICE * a, SLICE)
-        e = jnp.exp(jnp.dot(images, prs[a], preferred_element_type=F32) / TEMP)
-        ef[:, cols] = e
-        eh[:, cols] = e.astype(BF16)
-        cb[0, CUBE - 1, :, cols] = jnp.sum(e, axis=0, keepdims=True)
+
+    def scores(block):
+        images = zb[pl.ds(32 * block, 32)].astype(F32).reshape(128, 256).astype(BF16)
+        rows = pl.ds(128 * block, 128)
+        for a in range(4):
+            cols = pl.ds(SLICE * a, SLICE)
+            e = jnp.exp(jnp.dot(images, prs[a], preferred_element_type=F32) / TEMP)
+            ef[rows, cols] = e
+            eh[rows, cols] = e.astype(BF16)
+            column = jnp.sum(e, axis=0, keepdims=True)
+            cb[0, CUBE - 1, :, cols] = column if block else column + cb[0, CUBE - 1, :, cols]
+
+    wait(zb.at[pl.ds(32, 32)], d1_r.at[1])
+    scores(1)
+    wait(zb.at[pl.ds(1, 31)], d1_r.at[0])
+    scores(0)
 
     def total_of(sums):
         total = sums[0]
@@ -325,7 +336,7 @@
             dma((3,)), dma((3,)), dma,
             dma, dma,
             dma, dma,
-            dma, dma,
+            dma, dma((2,)),
             dma((SINK + 1,)), dma((SINK + 1,)),
             dma((SINK - 1,)), dma((SINK - 1,)),
             dma, dma,

time: 61.5 us -> 61 us (level)
  no operation moved by 1% of the time
where the time goes in v7:
time: 61 us; the launch traced here: 60.9 us
  Pallas kernels  60.2 us (99%)
  local copies, waits for them, and re-layouts  0.61 us (1%)
    pallas_call x1, Pallas kernels, shards(): pl.pallas_call(kernel, out_shape=jax.ShapeDtypeStruct((2, PROTOS), F32),...  60.2 us

profile of v7, /device:TPU:1, one launch (start us, length us, event | category | flops | bytes accessed | tf_op | source)
XLA Modules:
  0.0 60.9 jit_solution(15289443351606284155)
XLA Ops:
  0.0 60.2 %shard_map.46 = f32[2,3072]{1,0:T(2,128)S(1)} custom-call(bf16[14,14,2,512]{3,2,1,0:T(2,128)(2,1)} %bitcast.7, bf16[64,4608]{1,0:T(8,128)(2,1)} %bitcast.6, bf16[512,256]{1,0:T(8,128)(2,1)} %proj_hbm.1, bf16[256,384]{1,0:T(8,128)(2,1)} %proto_hbm.1), custom_call_target="tpu_custom_call" | custom-call | tf_op jit(solution)/shard_map/pallas_call | solution.py:311
  60.2 0.6 %copy.6 = f32[2,3072]{1,0:T(2,128)} copy(f32[2,3072]{1,0:T(2,128)S(1)} %shard_map.46) | data formatting | bytes 49152
